TPU v7x, 32 devices: a whole 2x2x4 slice. The times are simulated.
32 devices in a mesh: pipe: 4 (over y, core), ctx: 4 (over z), dp: 2 (over x).
Axes of the slice: x: 2, y: 2, z: 4, core: 2. Of those that a mesh axis runs over, the one named last changes fastest.
Arguments:
- hidden: bfloat16 [4, 1024, 4096], P('pipe', 'ctx', 'dp'), may hold values from -64 to 64
- cotangent: bfloat16 [4, 1024, 4096], P('pipe', 'ctx', 'dp'), may hold values from -6 to 6
- gain_rows: float32 [4, 4096], P('pipe', ('dp', 'ctx')), may hold values from 0.5 to 1.5
- short_taps: float32 [4, 9, 4096], P('pipe', None, ('dp', 'ctx')), may hold values from -3.5 to 3.5
- long_taps: float32 [4, 7, 4096], P('pipe', None, ('dp', 'ctx')), may hold values from -2 to 2
Outputs:
- hidden_grad: bfloat16 [4, 1024, 4096], P('pipe', 'ctx', 'dp')
- gain_grad: float32 [4, 4096], P('pipe', ('dp', 'ctx'))
- short_grad: float32 [4, 9, 4096], P('pipe', None, ('dp', 'ctx'))
- long_grad: float32 [4, 7, 4096], P('pipe', None, ('dp', 'ctx'))
All inputs are finite; a program needn't handle non-finite values.
Results may differ from a plain program's by a relative error of at most 0.0056.
Values may be sent and summed in bfloat16 or wider, within the bound.
A program may use at most 64 MiB of HBM per device.

v0:
```python
import jax
import jax.numpy as jnp
from jax import lax
from jax.sharding import PartitionSpec as P

WIDTH = 4096


def passed_along(value, axis, steps):
    count = lax.axis_size(axis)
    initial, last = (max(0, -steps), min(count, count - steps))
    return lax.ppermute(value, axis, [(source, source + steps) for source in range(initial, last)])


def shifted(value, axis, steps):
    count = lax.axis_size(axis)
    pairs = [(source, (source + steps) % count) for source in range(count)]
    return lax.ppermute(value, axis, pairs)


def delayed(source, places):
    if places == 0:
        return source
    zero_rows = jnp.zeros(source.shape[:-2] + (places, source.shape[-1]), source.dtype)
    return jnp.concatenate([zero_rows, source[..., : source.shape[-2] - places, :]], axis=-2)


def conv_branch(normed, short_filter, long_filter):
    tap_count = short_filter.shape[0] // 3
    lagged = [delayed(normed, tap_index) for tap_index in range(tap_count)]
    streams = []
    for stream_index in range(3):
        summed = short_filter[tap_count * stream_index] * lagged[0]
        for tap_index in range(1, tap_count):
            summed = summed + short_filter[tap_count * stream_index + tap_index] * lagged[tap_index]
        streams.append(summed)
    product = streams[1] * streams[2]
    mixing = long_filter[0] * product
    for tap_index in range(1, long_filter.shape[0]):
        mixing = mixing + long_filter[tap_index] * delayed(product, tap_index)
    return streams[0] * mixing


def row_total(values):
    return lax.psum(values, "dp")


def block_forward(values, filter_set):
    squares = row_total(jnp.sum(values * values, axis=-1))
    scale = lax.rsqrt(squares / WIDTH + 1e-05)[:, None]
    normed = values * scale * filter_set[0]
    branch, pull = jax.vjp(conv_branch, normed, filter_set[1], filter_set[2])
    return (values + branch, (values, scale, pull))


def block_backward(saved, filter_set, upstream):
    values, scale, pull = saved
    normed_grad, short_grad, long_grad = pull(upstream)
    gain_grad = jnp.sum(values * scale * normed_grad, axis=0)
    weighted = filter_set[0] * normed_grad
    projected = row_total(jnp.sum(values * weighted, axis=-1))[:, None]
    values_grad = upstream + scale * weighted - values * (scale * scale * scale / WIDTH) * projected
    return (values_grad, (gain_grad, short_grad, long_grad))


def pad_top(values, total_rows):
    zero_rows = jnp.zeros((total_rows - values.shape[0], values.shape[1]), values.dtype)
    return jnp.concatenate([zero_rows, values], axis=0)


def rows_across(values):
    return passed_along(values, "ctx", 1)


def grads_across(values):
    return passed_along(values, "ctx", -1)


def pipe_half(values, offset):
    return shifted(values, "pipe", offset)


def pipe_full(values, offset):
    return shifted(values, "pipe", offset)


def unpack_rows(filter_rows, short_count):
    return (filter_rows[0], filter_rows[1 : 1 + short_count], filter_rows[1 + short_count :])


def pack_rows(filter_set):
    return jnp.concatenate([filter_set[0][None, :], filter_set[1], filter_set[2]], axis=0)


def add_returned(local_grad, returned, depth):
    row_count = local_grad.shape[0] - depth
    zero_rows = jnp.zeros((row_count - depth, local_grad.shape[1]), jnp.float32)
    return local_grad[depth:] + jnp.concatenate([zero_rows, returned], axis=0)


def per_device(hidden, cotangent, gain_rows, short_taps, long_taps):
    row_count = hidden.shape[1]
    short_count = short_taps.shape[1]
    reach = short_count // 3 + long_taps.shape[1] - 2
    signal = hidden[0]
    cot_local = cotangent[0]
    packed = jnp.concatenate([gain_rows, short_taps[0], long_taps[0]], axis=0)
    filters = lax.all_gather(packed, "ctx", axis=1, tiled=True)
    first_filters = unpack_rows(filters, short_count)
    rim_rows = rows_across(signal[row_count - reach :]).astype(jnp.float32)
    signal_ext = jnp.concatenate([rim_rows, signal.astype(jnp.float32)], axis=0)
    first_out, first_saved = block_forward(signal_ext, first_filters)
    inner = first_out[signal_ext.shape[0] - row_count :].astype(jnp.bfloat16)
    arrived = pipe_half(inner, 1)
    inner_rim = rows_across(arrived[row_count - reach :]).astype(jnp.float32)
    second_ext = jnp.concatenate([inner_rim, arrived.astype(jnp.float32)], axis=0)
    second_out, second_saved = block_forward(second_ext, first_filters)
    second_up = pad_top(cot_local.astype(jnp.float32), second_ext.shape[0])
    inner_grad_ext, second_grads = block_backward(second_saved, first_filters, second_up)
    returned = grads_across(inner_grad_ext[:reach])
    inner_grad = add_returned(inner_grad_ext, returned, reach)
    inner_grad = pipe_full(inner_grad, -1)
    first_up = pad_top(inner_grad, signal_ext.shape[0])
    signal_grad_ext, first_grads = block_backward(first_saved, first_filters, first_up)
    returned_signal = grads_across(signal_grad_ext[:reach])
    hidden_grad = add_returned(signal_grad_ext, returned_signal, reach).astype(jnp.bfloat16)
    summed_grads = pack_rows(first_grads) + pack_rows(second_grads)
    reduced = lax.psum_scatter(summed_grads, "ctx", scatter_dimension=1, tiled=True)
    gain_grad = reduced[0:1]
    short_grad = reduced[1 : 1 + short_count][None]
    long_grad = reduced[1 + short_count :][None]
    return (hidden_grad[None], gain_grad, short_grad, long_grad)


def solution(mesh):
    in_specs = (
        P("pipe", "ctx", "dp"),
        P("pipe", "ctx", "dp"),
        P("pipe", ("dp", "ctx")),
        P("pipe", None, ("dp", "ctx")),
        P("pipe", None, ("dp", "ctx")),
    )
    out_specs = (
        P("pipe", "ctx", "dp"),
        P("pipe", ("dp", "ctx")),
        P("pipe", None, ("dp", "ctx")),
        P("pipe", None, ("dp", "ctx")),
    )
    return jax.shard_map(
        per_device, mesh=mesh, in_specs=in_specs, out_specs=out_specs, check_vma=False
    )
```

profile of v0, /device:TPU:0, one launch (start us, length us, event | category | flops | bytes accessed | tf_op | source)
XLA Modules:
  0.0 188.0 jit_solution(3203681902151841099)
XLA Ops:
  7.2 0.8 slice_bitcast_fusion
  8.1 4.9 %collective-permute-start = (bf16[8,2048]{1,0:T(8,128)(2,1)S(1)}, bf16[8,2048]{1,0:T(8,128)(2,1)S(1)}, u32[]{:S(2)}, u32[]{:S(2)}) collective-permute-start(bf16[8,2048]{1,0:T(8,128)(2,1)S(1)} %slice_bitcast_fusion), channel_id=1, source_target_pairs={{0,2},{2,4},{4,6},{1,3},{3,5},{5,7},{8,10},{10,12},{12,14},{9,11},... | collective-permute-start | bytes 98312 | tf_op jit(solution)/shard_map/ppermute | solution.py:12
  13.0 0.7 copy.14
  13.7 0.7 copy.13
  14.4 0.7 pad_maximum_fusion.2
  15.1 14.3 %all_gather.3 = f32[17,2048]{1,0:T(8,128)S(1)} all-gather(f32[17,512]{1,0:T(8,128)S(1)} %pad_maximum_fusion.2), channel_id=1, replica_groups=mesh['pipe'=4,'ctx'=4,'dp'=2] {'ctx'}, dimensions={1}, use_global_device_ids=true | all-gather | bytes 174080 | tf_op jit(solution)/shard_map/all_gather | solution.py:108
  29.5 1.5 multiply_reduce_fusion.34
  31.0 4.9 %psum.28 = f32[264]{0:T(512)S(1)} all-reduce(f32[264]{0:T(512)S(1)} %multiply_reduce_fusion.34), channel_id=1, replica_groups=mesh['pipe'=4,'ctx'=4,'dp'=2] {'dp'}, use_global_device_ids=true, to_apply=%region_1.0 | all-reduce | flops 264 | bytes 2112 | tf_op jit(solution)/shard_map/psum | solution.py:45
  36.0 0.6 fusion.20
  36.6 0.3 fusion.15
  36.8 1.7 multiply_add_fusion.7
  38.6 2.0 %multiply_add_fusion.4 = f32[264,2048]{1,0:T(8,128)S(1)} fusion(f32[264,2048]{1,0:T(8,128)S(1)} %get-tuple-element.51, f32[258,2048]{1,0:T(8,128)S(1)} %bitcast.91, f32[259,2048]{1,0:T(8,128)S(1)} %bitcast.92, f32[260,2048]{1,0:T(8,128)S(1)} %bitcast.93, f32[261,2048]{1,0:T(8,128)S(1)} %bitcast.94, f32[262,2048]{1,0:T(8,128)S(1)} %bitcast.95, ...), kind=kLoop, calls=%fused_computation.87 | loop fusion | flops 7028736 | bytes 17186816 | tf_op jit(solution)/shard_map/jvp()/add | solution.py:40
  40.9 0.6 fusion.17
  41.5 0.4 copy-done.6
  41.9 14.2 %collective-permute-done.1 = bf16[256,2048]{1,0:T(8,128)(2,1)S(1)} collective-permute-done((bf16[256,2048]{1,0:T(8,128)(2,1)S(1)}, bf16[256,2048]{1,0:T(8,128)(2,1)S(1)}, u32[]{:S(2)}, u32[]{:S(2)}) %collective-permute-start.1) | collective-permute-done | bytes 1048608 | tf_op jit(solution)/shard_map/ppermute | solution.py:18
  56.2 1.3 collective-permute-start.2
  57.4 1.6 collective-permute-done.2
  59.0 0.3 fusion.4
  59.3 5.1 %psum.29 = f32[264]{0:T(512)S(1)} all-reduce(f32[264]{0:T(512)S(1)} %fusion.4), channel_id=1, replica_groups=mesh['pipe'=4,'ctx'=4,'dp'=2] {'dp'}, use_global_device_ids=true, to_apply=%region_3.0 | all-reduce | flops 264 | bytes 2112 | tf_op jit(solution)/shard_map/psum | solution.py:45
  64.5 0.3 fusion.1
  64.8 1.4 fusion.24
  66.1 4.7 %multiply_reduce_fusion.6 = (f32[2048]{0:T(1024)S(1)}, f32[2048]{0:T(1024)S(1)}, f32[2048]{0:T(1024)S(1)}, f32[2048]{0:T(1024)S(1)}, f32[2048]{0:T(1024)S(1)}, /...) fusion(f32[258,2048]{1,0:T(8,128)S(1)} %bitcast.79, f32[264,2048]{1,0:T(8,128)S(1)} %fusion.24, ...), kind=kLoop, calls=%fused_computation.52 | loop fusion | flops 14583808 | bytes 23651360 | tf_op jit(solution)/shard_map/transpose(jvp())/reduce_sum | solution.py:40
  70.8 0.3 slice_multiply_fusion.18
  71.2 0.4 slice_multiply_fusion.19
  71.5 0.4 slice_multiply_fusion.20
  71.9 0.4 slice_multiply_fusion.21
  72.2 0.4 slice_multiply_fusion.22
  72.6 0.4 slice_multiply_fusion.23
  73.0 6.8 %multiply_reduce_fusion.15 = (f32[2048]{0:T(1024)S(1)}, f32[2048]{0:T(1024)S(1)}, f32[2048]{0:T(1024)S(1)}, f32[2048]{0:T(1024)S(1)}, f32[2048]{0:T(1024)}, /*in...) fusion(f32[262,2048]{1,0:T(8,128)S(1)} %bitcast.107, ...), kind=kLoop, calls=%fused_computation.61 | loop fusion | flops 31340544 | bytes 43041824 | tf_op jit(solution)/shard_map/transpose(jvp())/reduce_sum | solution.py:35
  79.8 0.8 fusion.11
  80.6 0.9 fusion.13
  81.5 2.5 %fusion.2 = (f32[2048]{0:T(1024)S(1)}, f32[264]{0:T(512)S(1)}, f32[264,2048]{1,0:T(8,128)}) fusion(f32[264]{0:T(512)S(1)} %get-tuple-element.72, bf16[256,2048]{1,0:T(8,128)(2,1)S(1)} %collective-permute-done.1, bf16[8,2048]{1,0:T(8,128)(2,1)S(1)} %collective-permute-done.2, f32[2048]{0:T(1024)S(1)} %bitcast.129, f32[263,2048]{1,0:T(8,128)S(1)} %fusion.11, ...), kind=kLoop, calls=%fused_computation.9 | loop fusion | flops 9189112 | bytes 14075968 | tf_op jit(solution)/shard_map/reduce_sum | solution.py:59
  84.0 4.9 %psum.30 = f32[264]{0:T(512)S(1)} all-reduce(f32[264]{0:T(512)S(1)} %get-tuple-element.5), channel_id=1, replica_groups=mesh['pipe'=4,'ctx'=4,'dp'=2] {'dp'}, use_global_device_ids=true, to_apply=%region_5.0 | all-reduce | flops 264 | bytes 2112 | tf_op jit(solution)/shard_map/psum | solution.py:45
  89.0 2.5 %fusion.3 = f32[264,2048]{1,0:T(8,128)S(1)} fusion(f32[264,2048]{1,0:T(8,128)} %get-tuple-element.49, f32[264]{0:T(512)S(1)} %psum.30, f32[264]{0:T(512)S(1)} %get-tuple-element.71, f32[264]{0:T(512)S(1)} %get-tuple-element.72, f32[2048]{0:T(1024)S(1)} %bitcast.130, bf16[256,2048]{1,0:T(8,128)(2,1)} %bitcast.120, ...), kind=kLoop, calls=%fused_computation.10 | loop fusion | flops 5947392 | bytes 6466656 | tf_op jit(solution)/shard_map/sub | solution.py:62
  91.5 1.4 collective-permute-start.3
  92.9 5.2 %collective-permute-done.3 = f32[8,2048]{1,0:T(8,128)S(1)} collective-permute-done((f32[8,2048]{1,0:T(8,128)S(1)}, f32[8,2048]{1,0:T(8,128)S(1)}, u32[]{:S(2)}, u32[]{:S(2)}) %collective-permute-start.3) | collective-permute-done | bytes 65568 | tf_op jit(solution)/shard_map/ppermute | solution.py:12
  98.3 0.3 collective-permute-start.4
  98.5 23.5 %collective-permute-done.4 = f32[256,2048]{1,0:T(8,128)S(1)} collective-permute-done((f32[256,2048]{1,0:T(8,128)S(1)}, f32[256,2048]{1,0:T(8,128)S(1)}, u32[]{:S(2)}, u32[]{:S(2)}) %collective-permute-start.4) | collective-permute-done | bytes 2097184 | tf_op jit(solution)/shard_map/ppermute | solution.py:18
  122.1 2.6 %multiply_reduce_fusion.22 = (f32[2048]{0:T(1024)S(1)}, f32[2048]{0:T(1024)S(1)}, f32[2048]{0:T(1024)S(1)}, f32[2048]{0:T(1024)S(1)}, f32[2048]{0:T(1024)S(1)}, ...) fusion(f32[258,2048]{1,0:T(8,128)S(1)} %bitcast.97, f32[264,2048]{1,0:T(8,128)S(1)} %get-tuple-element.51, ...), kind=kLoop, calls=%fused_computation.68 | loop fusion | flops 8095744 | bytes 21446656 | tf_op jit(solution)/shard_map/transpose(jvp())/reduce_sum | solution.py:40
  124.7 0.3 slice_multiply_fusion.6
  125.1 0.4 slice_multiply_fusion.7
  125.5 0.3 slice_multiply_fusion.8
  125.8 1.8 slice_multiply_fusion.9
  127.5 1.8 slice_multiply_fusion.10
  129.3 1.8 slice_multiply_fusion.11
  131.1 0.4 copy-done.1
  131.5 0.5 copy-done.3
  132.0 7.2 %multiply_reduce_fusion.31 = (f32[2048]{0:T(1024)S(1)}, f32[2048]{0:T(1024)S(1)}, f32[2048]{0:T(1024)S(1)}, f32[2048]{0:T(1024)S(1)}, f32[2048]{0:T(1024)S(1)}, ...) fusion(f32[262,2048]{1,0:T(8,128)S(1)} %bitcast.111, ...), kind=kLoop, calls=%fused_computation.77 | loop fusion | flops 23771136 | bytes 31237152 | tf_op jit(solution)/shard_map/transpose(jvp())/reduce_sum | solution.py:35
  139.2 0.8 fusion.7
  140.0 0.8 fusion.9
  140.9 2.6 %multiply_reduce_fusion.32 = (f32[2048]{0:T(1024)S(1)}, f32[264]{0:T(512)S(1)}, f32[264,2048]{1,0:T(8,128)}) fusion(f32[264]{0:T(512)S(1)} %get-tuple-element.70, bf16[256,2048]{1,0:T(8,128)(2,1)S(1)} %bitcast.118, bf16[8,2048]{1,0:T(8,128)(2,1)S(1)} %collective-permute-done, f32[2048]{0:T(1024)S(1)} %bitcast.132, f32[263,2048]{1,0:T(8,128)S(1)} %fusion.7, ...), kind=kLoop, calls=%fused_computation.78 | loop fusion | flops 9189112 | bytes 14075968 | tf_op jit(solution)/shard_map/reduce_sum | solution.py:59
  143.4 4.9 %psum.31 = f32[264]{0:T(512)S(1)} all-reduce(f32[264]{0:T(512)S(1)} %get-tuple-element.7), channel_id=1, replica_groups=mesh['pipe'=4,'ctx'=4,'dp'=2] {'dp'}, use_global_device_ids=true, to_apply=%region_7.0 | all-reduce | flops 264 | bytes 2112 | tf_op jit(solution)/shard_map/psum | solution.py:45
  148.4 2.3 %multiply_subtract_fusion = f32[264,2048]{1,0:T(8,128)S(1)} fusion(f32[264,2048]{1,0:T(8,128)} %get-tuple-element.48, f32[256,2048]{1,0:T(8,128)S(1)} %copy-done.9, f32[264]{0:T(512)S(1)} %psum.31, f32[264]{0:T(512)S(1)} %copy-done.20, f32[2048]{0:T(1024)S(1)} %bitcast.133, f32[264]{0:T(512)S(1)} %get-tuple-element.70, bf16[256,2048]{1,0:T(8,128)(2,1)S(1)} %bitcast.119, ...), kind=kLoop, calls=%fused_computation.79 | loop fusion | flops 5406720 | bytes 7515232 | tf_op jit(solution)/shard_map/sub | solution.py:62
  150.7 1.3 copy-done.11
  152.0 1.3 collective-permute-start.5
  153.8 0.8 maximum_add_fusion
  154.5 4.3 %collective-permute-done.5 = f32[8,2048]{1,0:T(8,128)S(1)} collective-permute-done((f32[8,2048]{1,0:T(8,128)S(1)}, f32[8,2048]{1,0:T(8,128)S(1)}, u32[]{:S(2)}, u32[]{:S(2)}) %collective-permute-start.5) | collective-permute-done | bytes 65568 | tf_op jit(solution)/shard_map/ppermute | solution.py:12
  158.8 2.7 %fusion.18 = bf16[1,256,2048]{2,1,0:T(8,128)(2,1)} fusion(f32[8,2048]{1,0:T(8,128)S(1)} %collective-permute-done.5, f32[264,2048]{1,0:T(8,128)} %copy-done.11), kind=kLoop, calls=%fused_computation.104 | loop fusion | flops 1048576 | bytes 3211264 | tf_op jit(solution)/shard_map/broadcast_in_dim | solution.py:132
  161.6 15.5 %reduce-scatter.2.cloned.1.call-done = f32[17,512]{1,0:T(8,128)} async-done(((f32[17,2048]{1,0:T(8,128)}), f32[17,512]{1,0:T(8,128)}) %reduce-scatter.2.cloned.1.call-update) | async-done | bytes 34832 | tf_op jit(solution)/shard_map/reduce_scatter | solution.py:128
  177.1 0.8 slice.253
  177.9 0.6 broadcast_in_dim.13
  178.5 0.8 slice.254
  179.3 0.6 broadcast_in_dim.14
  179.9 1.3 slice.252
  (51 shorter events, 1.0 us)
Async XLA Ops:
  7.2 29.4 %copy-start.2 = (bf16[1,256,2048]{2,1,0:T(8,128)(2,1)S(1)}, bf16[1,256,2048]{2,1,0:T(8,128)(2,1)}, u32[]{:S(2)}) copy-start(bf16[1,256,2048]{2,1,0:T(8,128)(2,1)} %param.5) | copy-start | bytes 3145732
  7.2 169.9 %reduce-scatter.2.cloned.1.call-start = ((), (), s32[]{:S(2)}) async-start(), calls=%async_computation.1 | async-start | bytes 245760 | tf_op jit(solution)/shard_map/reduce_scatter | solution.py:128
  8.1 21.4 %collective-permute-start = (bf16[8,2048]{1,0:T(8,128)(2,1)S(1)}, bf16[8,2048]{1,0:T(8,128)(2,1)S(1)}, u32[]{:S(2)}, u32[]{:S(2)}) collective-permute-start(bf16[8,2048]{1,0:T(8,128)(2,1)S(1)} %slice_bitcast_fusion), channel_id=1, source_target_pairs={{0,2},{2,4},{4,6},{1,3},{3,5},{5,7},{8,10},{10,12},{12,14},{9,11},... | collective-permute-start | bytes 98312 | tf_op jit(solution)/shard_map/ppermute | solution.py:12
  36.8 1.7 copy-start
  38.6 2.3 %copy-start.4 = (f32[264,2048]{1,0:T(8,128)}, f32[264,2048]{1,0:T(8,128)S(1)}, u32[]{:S(2)}) copy-start(f32[264,2048]{1,0:T(8,128)S(1)} %get-tuple-element.50) | copy-start | bytes 6488068
  40.6 1.3 copy-start.6
  41.9 14.2 %collective-permute-start.1 = (bf16[256,2048]{1,0:T(8,128)(2,1)S(1)}, bf16[256,2048]{1,0:T(8,128)(2,1)S(1)}, u32[]{:S(2)}, u32[]{:S(2)}) collective-permute-start(bf16[256,2048]{1,0:T(8,128)(2,1)S(1)} %fusion.17), channel_id=1, source_target_pairs={{0,8},{8,16},{16,24},{24,0},{1,9},{9,17},{17,25},{25,1},{2,10},{10... | collective-permute-start | bytes 3145736 | tf_op jit(solution)/shard_map/ppermute | solution.py:18
  56.2 2.9 %collective-permute-start.2 = (bf16[8,2048]{1,0:T(8,128)(2,1)S(1)}, bf16[8,2048]{1,0:T(8,128)(2,1)S(1)}, u32[]{:S(2)}, u32[]{:S(2)}) collective-permute-start(bf16[8,2048]{1,0:T(8,128)(2,1)S(1)} %slice.239), channel_id=1, source_target_pairs={{0,2},{2,4},{4,6},{1,3},{3,5},{5,7},{8,10},{10,12},{12,14},{9,11},... | collective-permute-start | bytes 98312 | tf_op jit(solution)/shard_map/ppermute | solution.py:12
  64.7 1.4 copy-start.10
  91.5 30.6 %copy-start.5 = (f32[264,2048]{1,0:T(8,128)S(1)}, f32[264,2048]{1,0:T(8,128)}, u32[]{:S(2)}) copy-start(f32[264,2048]{1,0:T(8,128)} %copy-done.4) | copy-start | bytes 6488068
  91.5 6.6 %collective-permute-start.3 = (f32[8,2048]{1,0:T(8,128)S(1)}, f32[8,2048]{1,0:T(8,128)S(1)}, u32[]{:S(2)}, u32[]{:S(2)}) collective-permute-start(f32[8,2048]{1,0:T(8,128)S(1)} %slice.249), channel_id=1, source_target_pairs={{2,0},{4,2},{6,4},{3,1},{5,3},{7,5},{10,8},{12,10},{14,12},{11,9},... | collective-permute-start | bytes 196616 | tf_op jit(solution)/shard_map/ppermute | solution.py:12
  98.3 23.8 %collective-permute-start.4 = (f32[256,2048]{1,0:T(8,128)S(1)}, f32[256,2048]{1,0:T(8,128)S(1)}, u32[]{:S(2)}, u32[]{:S(2)}) collective-permute-start(f32[256,2048]{1,0:T(8,128)S(1)} %slice_add_fusion.1), channel_id=1, source_target_pairs={{0,24},{8,0},{16,8},{24,16},{1,25},{9,1},{17,9},{25,17},{2,26},{10... | collective-permute-start | bytes 6291464 | tf_op jit(solution)/shard_map/ppermute | solution.py:18
  122.1 9.0 %copy-start.8 = (f32[256,2048]{1,0:T(8,128)}, f32[256,2048]{1,0:T(8,128)S(1)}, u32[]{:S(2)}) copy-start(f32[256,2048]{1,0:T(8,128)S(1)} %collective-permute-done.4) | copy-start | bytes 6291460
  127.5 3.6 %copy-start.7 = (f32[264,2048]{1,0:T(8,128)S(1)}, f32[264,2048]{1,0:T(8,128)}, u32[]{:S(2)}) copy-start(f32[264,2048]{1,0:T(8,128)} %copy-done.6) | copy-start | bytes 6488068
  129.3 2.3 %copy-start.1 = (f32[264,2048]{1,0:T(8,128)S(1)}, f32[264,2048]{1,0:T(8,128)}, u32[]{:S(2)}) copy-start(f32[264,2048]{1,0:T(8,128)} %copy-done) | copy-start | bytes 6488068
  129.3 2.8 %copy-start.3 = (bf16[1,256,2048]{2,1,0:T(8,128)(2,1)S(1)}, bf16[1,256,2048]{2,1,0:T(8,128)(2,1)}, u32[]{:S(2)}) copy-start(bf16[1,256,2048]{2,1,0:T(8,128)(2,1)} %param.5) | copy-start | bytes 3145732
  140.8 7.5 %copy-start.9 = (f32[256,2048]{1,0:T(8,128)S(1)}, f32[256,2048]{1,0:T(8,128)}, u32[]{:S(2)}) copy-start(f32[256,2048]{1,0:T(8,128)} %copy-done.8) | copy-start | bytes 6291460
  140.8 7.5 %copy-start.20 = (f32[264]{0:T(512)S(1)}, f32[264]{0:T(512)}, u32[]{:S(2)}) copy-start(f32[264]{0:T(512)} %get-tuple-element.69) | copy-start | bytes 3172
  148.3 5.1 %copy-start.12 = (f32[2048]{0:T(1024)S(1)}, f32[2048]{0:T(1024)}, u32[]{:S(2)}) copy-start(f32[2048]{0:T(1024)} %get-tuple-element.12) | copy-start | bytes 24580
  148.3 5.1 %copy-start.13 = (f32[2048]{0:T(1024)S(1)}, f32[2048]{0:T(1024)}, u32[]{:S(2)}) copy-start(f32[2048]{0:T(1024)} %get-tuple-element.13) | copy-start | bytes 24580
  148.3 5.1 %copy-start.14 = (f32[2048]{0:T(1024)S(1)}, f32[2048]{0:T(1024)}, u32[]{:S(2)}) copy-start(f32[2048]{0:T(1024)} %get-tuple-element.14) | copy-start | bytes 24580
  148.4 5.1 %copy-start.15 = (f32[2048]{0:T(1024)S(1)}, f32[2048]{0:T(1024)}, u32[]{:S(2)}) copy-start(f32[2048]{0:T(1024)} %get-tuple-element.15) | copy-start | bytes 24580
  148.4 5.1 %copy-start.16 = (f32[2048]{0:T(1024)S(1)}, f32[2048]{0:T(1024)}, u32[]{:S(2)}) copy-start(f32[2048]{0:T(1024)} %get-tuple-element.16) | copy-start | bytes 24580
  148.4 5.1 %copy-start.17 = (f32[2048]{0:T(1024)S(1)}, f32[2048]{0:T(1024)}, u32[]{:S(2)}) copy-start(f32[2048]{0:T(1024)} %get-tuple-element.30) | copy-start | bytes 24580
  148.4 5.1 %copy-start.18 = (f32[2048]{0:T(1024)S(1)}, f32[2048]{0:T(1024)}, u32[]{:S(2)}) copy-start(f32[2048]{0:T(1024)} %get-tuple-element.31) | copy-start | bytes 24580
  148.4 5.1 %copy-start.19 = (f32[2048]{0:T(1024)S(1)}, f32[2048]{0:T(1024)}, u32[]{:S(2)}) copy-start(f32[2048]{0:T(1024)} %get-tuple-element.32) | copy-start | bytes 24580
  150.7 1.4 copy-start.11
  152.0 6.8 %collective-permute-start.5 = (f32[8,2048]{1,0:T(8,128)S(1)}, f32[8,2048]{1,0:T(8,128)S(1)}, u32[]{:S(2)}, u32[]{:S(2)}) collective-permute-start(f32[8,2048]{1,0:T(8,128)S(1)} %slice.251), channel_id=1, source_target_pairs={{2,0},{4,2},{6,4},{3,1},{5,3},{7,5},{10,8},{12,10},{14,12},{11,9},... | collective-permute-start | bytes 196616 | tf_op jit(solution)/shard_map/ppermute | solution.py:12
Sparse Core Ops, SparseCore 0:
  154.7 22.3 reduce-scatter.1
where the time goes:
time: 189 us; the launch traced here: 188 us
  waiting for transfers between devices  64.3 us (34%)
  other arithmetic  56.5 us (30%)
  blocking collectives  34.2 us (18%)
  between operations  14.5 us (8%)
  local copies, waits for them, and re-layouts  9.25 us (5%)
  starting transfers between devices  9.22 us (5%)
    ppermute x2, waiting for transfers between devices, shifted(): return lax.ppermute(value, axis, pairs)  37.8 us
    psum x4, blocking collectives, row_total(): return lax.psum(values, 'dp')  19.9 us
    reduce_scatter x1, waiting for transfers between devices, per_device(): lax.psum_scatter(summed_grads, 'ctx', scatter_dimension=1, tiled=True)  15.5 us
    all_gather x1, blocking collectives, per_device(): filters = lax.all_gather(packed, 'ctx', axis=1, tiled=True)  14.3 us
    reduce_sum x2, other arithmetic, conv_branch(): short_filter[tap_count * stream_index + tap_index] * lagged[tap_index]  14 us
    ppermute x4, waiting for transfers between devices, passed_along(): lax.ppermute(value, axis, [(source, source + steps) for source in range(i...  11 us
    ppermute x4, starting transfers between devices, passed_along(): lax.ppermute(value, axis, [(source, source + steps) for source in range(i...  8.9 us
    mul x12, other arithmetic, conv_branch(): mixing = mixing + long_filter[tap_index] * delayed(product, tap_index)  8.45 us
  transfers between devices with their start and end apart: 7, of which 6 were waited for; matrix products, arithmetic and copies ran while one was open for 3% of the time, Pallas kernels for 0%

commit v1 on v0

v1 whole, which is shorter than its diff:
```python
import functools

import jax
import jax.numpy as jnp
from jax import lax
from jax.experimental import pallas as pl
from jax.experimental.pallas import tpu as pltpu
from jax.sharding import PartitionSpec as P

MESH = pl.DeviceIdType.MESH
F32 = jnp.float32
BF16 = jnp.bfloat16
LANES = 128
SUB = 8
EPS = 1e-05


def kernel(
    cfg,
    hid,
    cot,
    gain_in,
    short_in,
    long_in,
    out,
    gain_out,
    short_out,
    long_out,
    hbuf,
    htop,
    hbot,
    cbuf,
    cbot,
    slab,
    fr,
    filt,
    grads,
    gs,
    rg,
    xs,
    zs,
    wd,
    saved,
    parts,
    st_send,
    st_recv,
    rows,
    blank,
    loc_sem,
    halo_send,
    halo_recv,
    f_send,
    f_recv,
    g_send,
    g_recv,
    s_send,
    s_recv,
):
    npipe, nctx, ndp = cfg["npipe"], cfg["nctx"], cfg["ndp"]
    nrow, nb, cb, ntap, nshort, width = (
        cfg["nrow"], cfg["nb"], cfg["cb"], cfg["ntap"], cfg["nshort"], cfg["width"],
    )
    taps = nshort // 3
    nlong = ntap - 1 - nshort
    halo = cfg["halo"]
    total = nrow + 2 * halo
    groups = nb // SUB
    nstat = total // SUB
    pipe, ctx, dp = lax.axis_index("pipe"), lax.axis_index("ctx"), lax.axis_index("dp")
    prev = lax.rem(pipe + npipe - 1, npipe)
    follow = lax.rem(pipe + 1, npipe)

    def ctx_at(o):
        return lax.rem(ctx + o, nctx)

    def dp_at(o):
        return lax.rem(dp + o, ndp)

    def dev(p, z, d):
        return {"pipe": p, "ctx": z, "dp": d}

    def remote(src, dst, ss, rs, where):
        return pltpu.make_async_remote_copy(
            src_ref=src, dst_ref=dst, send_sem=ss, recv_sem=rs, device_id=where, device_id_type=MESH
        )

    load_hid = pltpu.make_async_copy(hid.at[0], hbuf, loc_sem.at[0])
    load_hid.start()
    blank[...] = jnp.zeros((SUB, LANES), F32)

    for k in range(ntap):
        src, row = (gain_in, 0) if k == 0 else ((short_in, k - 1) if k <= nshort else (long_in, k - 1 - nshort))
        for j in range(cb):
            cols = pl.ds(j * LANES, LANES)
            piece = src[row : row + 1, cols] if k == 0 else src[0, row : row + 1, cols]
            slab[k * cb + j : k * cb + j + 1, :] = piece
    pad = slab.shape[0] - ntap * cb
    if pad:
        slab[ntap * cb :, :] = jnp.zeros((pad, LANES), F32)
        for b in range(2):
            for z in range(nctx):
                gs[b, z, ntap * cb :, :] = jnp.zeros((pad, LANES), F32)
    fr[0, ctx] = slab[...]

    barrier = pltpu.get_barrier_semaphore()
    greeted = 0
    for p in (pipe, prev, follow):
        for o in range(nctx):
            if p is pipe and o == 0:
                continue
            pl.semaphore_signal(barrier, inc=1, device_id=dev(p, ctx_at(o), dp), device_id_type=MESH)
            greeted += 1
    for o in range(1, ndp):
        pl.semaphore_signal(barrier, inc=1, device_id=dev(pipe, ctx, dp_at(o)), device_id_type=MESH)
        greeted += 1
    pl.semaphore_wait(barrier, greeted)

    up_z = lax.max(ctx - 1, 0)
    down_z = lax.min(ctx + 1, nctx - 1)
    head, tail = pl.ds(0, halo), pl.ds(nrow - halo, halo)
    to_bot = remote(hid.at[0, head, :], hbot, halo_send.at[0], halo_recv.at[0], dev(pipe, up_z, dp))
    to_top = remote(hid.at[0, tail, :], htop, halo_send.at[1], halo_recv.at[1], dev(pipe, down_z, dp))
    to_cbot = remote(cot.at[0, head, :], cbot, halo_send.at[2], halo_recv.at[2], dev(prev, up_z, dp))
    to_cot = remote(cot.at[0], cbuf, halo_send.at[3], halo_recv.at[3], dev(prev, ctx, dp))
    has_up, has_down = ctx > 0, ctx < nctx - 1

    @pl.when(has_up)
    def _():
        to_bot.start()

    @pl.when(has_down)
    def _():
        to_top.start()

    own_sends = []
    for o in range(1, nctx):
        own_sends.append(
            remote(slab, fr.at[0, ctx], f_send.at[0, o], f_recv.at[0, ctx], dev(pipe, ctx_at(o), dp))
        )
    for o in range(nctx):
        own_sends.append(
            remote(slab, fr.at[1, ctx], f_send.at[1, o], f_recv.at[1, ctx], dev(prev, ctx_at(o), dp))
        )
    for c in own_sends:
        c.start()

    @pl.when(has_up)
    def _():
        to_cbot.start()

    to_cot.start()

    lane = lax.broadcasted_iota(jnp.int32, (SUB, LANES), 1)

    def spread(dst, first, block):
        for half in range(2):
            piece = block[half * SUB : (half + 1) * SUB, :]
            start = (first + half * SUB) * nb
            for j in range(nb):
                dst[pl.ds(start + j, SUB, stride=nb), :] = piece[:, j * LANES : (j + 1) * LANES]

    def squares(stat, first, block):
        for half in range(2):
            acc = None
            for j in range(nb):
                piece = block[half * SUB : (half + 1) * SUB, j * LANES : (j + 1) * LANES]
                acc = piece * piece if acc is None else acc + piece * piece
            value = jnp.sum(acc, axis=1, keepdims=True)
            stat = jnp.where(lane == first // SUB + half, value, stat)
        return stat

    load_hid.wait()

    def take_hidden(i, stat):
        block = hbuf[pl.ds(pl.multiple_of(i * 16, 16), 16), :].astype(F32)
        spread(xs, halo + i * 16, block)
        return squares(stat, halo + i * 16, block)

    stat = lax.fori_loop(0, nrow // 16, take_hidden, jnp.zeros((SUB, LANES), F32))

    @pl.when(has_down)
    def _():
        remote(hbot, hbot, halo_send.at[0], halo_recv.at[0], dev(pipe, down_z, dp)).wait_recv()

    @pl.when(jnp.logical_not(has_down))
    def _():
        hbot[...] = jnp.zeros(hbot.shape, BF16)

    @pl.when(has_up)
    def _():
        remote(htop, htop, halo_send.at[1], halo_recv.at[1], dev(pipe, up_z, dp)).wait_recv()

    @pl.when(jnp.logical_not(has_up))
    def _():
        htop[...] = jnp.zeros(htop.shape, BF16)

    for first, ref in ((0, htop), (halo + nrow, hbot)):
        block = ref[...].astype(F32)
        spread(xs, first, block)
        stat = squares(stat, first, block)

    def send_stat(stage, value):
        st_send[stage] = value
        st_recv[stage, dp] = value
        for o in range(1, ndp):
            remote(
                st_send.at[stage], st_recv.at[stage, dp], s_send.at[stage, o], s_recv.at[stage, dp],
                dev(pipe, ctx, dp_at(o)),
            ).start()

    def get_stat(stage):
        for o in range(1, ndp):
            there = dp_at(o)
            remote(
                st_send.at[stage], st_recv.at[stage, there], s_send.at[stage, o], s_recv.at[stage, there],
                dev(pipe, ctx, there),
            ).wait()
        value = st_recv[stage, 0]
        for d in range(1, ndp):
            value = value + st_recv[stage, d]
        return value

    def unpack(stage, value, fn):
        for i in range(nstat):
            column = jnp.sum(jnp.where(lane == i, value, 0.0), axis=1, keepdims=True)
            rows[stage, i * SUB : (i + 1) * SUB, :] = jnp.broadcast_to(fn(column), (SUB, LANES))

    def collect(lo, hi):
        def step(i, stat):
            acc = None
            for g in range(groups):
                base = (g * total + i * SUB) * SUB
                for k in range(SUB):
                    piece = parts[pl.ds(base + k, SUB, stride=SUB), :]
                    acc = piece if acc is None else acc + piece
            return jnp.where(lane == i, jnp.sum(acc, axis=1, keepdims=True), stat)

        return lax.fori_loop(lo, hi, step, jnp.zeros((SUB, LANES), F32))

    def build_filters(b):
        for z in range(nctx):
            for k in range(ntap):
                filt[b, k * nb + z * cb : k * nb + (z + 1) * cb, :] = fr[b, z, k * cb : (k + 1) * cb, :]

    def row_scale(value):
        return lax.rsqrt(value / width + EPS)

    send_stat(0, stat)
    for o in range(1, nctx):
        there = ctx_at(o)
        remote(slab, fr.at[0, there], f_send.at[0, o], f_recv.at[0, there], dev(pipe, there, dp)).wait_recv()
    build_filters(0)
    unpack(0, get_stat(0), row_scale)

    def at(w, g):
        return pl.ds(pl.multiple_of(w * nb + g * SUB, SUB), SUB)

    def row_of(stage, w):
        return jnp.broadcast_to(rows[stage, pl.ds(w, 1), :], (SUB, LANES))

    def tap(b, k, g):
        return filt[b, pl.ds(pl.multiple_of(k * nb + g * SUB, SUB), SUB), :]

    def forward(b, lo, unroll):
        def group(g, _):
            fl = [tap(b, k, g) for k in range(ntap)]
            gain, short, long = fl[0], fl[1 : 1 + nshort], fl[1 + nshort :]

            def step(it, carry):
                lag = list(carry[: taps - 1])
                past = list(carry[taps - 1 :])
                for u in range(unroll):
                    w = lo + it * unroll + u
                    x = xs[at(w, g), :]
                    xh = x * row_of(b, w)
                    seq = [xh * gain] + lag
                    streams = []
                    for j in range(3):
                        value = short[taps * j] * seq[0]
                        for i in range(1, taps):
                            value = value + short[taps * j + i] * seq[i]
                        streams.append(value)
                    products = [streams[1] * streams[2]] + past
                    mix = long[0] * products[0]
                    for i in range(1, nlong):
                        mix = mix + long[i] * products[i]
                    for n, value in enumerate((xh, streams[0], streams[1], streams[2], mix)):
                        saved[b, n, at(w, g), :] = value
                    if b == 0:
                        inner = (x + streams[0] * mix).astype(BF16).astype(F32)
                        xs[at(w, g), :] = inner
                        spot = pl.multiple_of((g * total + w) * SUB, SUB)
                        parts[pl.ds(spot, SUB), :] = inner * inner
                    lag, past = seq[:-1], products[:-1]
                return tuple(lag + past)

            zero = blank[...]
            lax.fori_loop(0, (total - lo) // unroll, step, (zero,) * (taps - 1 + nlong - 1))
            return 0

        lax.fori_loop(0, groups, group, 0)

    forward(0, 0, 8)
    send_stat(1, collect(0, nstat))

    remote(cbuf, cbuf, halo_send.at[3], halo_recv.at[3], dev(follow, ctx, dp)).wait_recv()

    @pl.when(has_down)
    def _():
        remote(cbot, cbot, halo_send.at[2], halo_recv.at[2], dev(follow, down_z, dp)).wait_recv()

    @pl.when(jnp.logical_not(has_down))
    def _():
        cbot[...] = jnp.zeros(cbot.shape, BF16)

    def take_cot(i, _):
        spread(zs, halo + i * 16, cbuf[pl.ds(pl.multiple_of(i * 16, 16), 16), :].astype(F32))
        return 0

    lax.fori_loop(0, nrow // 16, take_cot, 0)
    spread(zs, halo + nrow, cbot[...].astype(F32))
    for z in range(nctx):
        remote(slab, fr.at[1, z], f_send.at[1, z], f_recv.at[1, z], dev(follow, z, dp)).wait_recv()
    build_filters(1)
    unpack(1, get_stat(1), row_scale)
    forward(1, halo // 2, 8)

    def backward(b, top, unroll):
        def group(g, _):
            fl = [tap(b, k, g) for k in range(ntap)]
            gain, short, long = fl[0], fl[1 : 1 + nshort], fl[1 + nshort :]

            def one(w, state, acc):
                dmix_next, ds_next = state
                here = at(w, g)
                up = zs[here, :]
                if b == 0:
                    up = up + row_of(1, w) * (wd[here, :] - saved[1, 0, here, :] * row_of(2, w))
                    zs[here, :] = up
                xh, query, key, value, mix = [saved[b, n, here, :] for n in range(5)]
                dmix = [up * query] + dmix_next
                dprod = long[0] * dmix[0]
                for i in range(1, nlong):
                    dprod = dprod + long[i] * dmix[i]
                ds = [[up * mix] + ds_next[0], [dprod * value] + ds_next[1], [dprod * key] + ds_next[2]]
                dn = None
                for j in range(3):
                    for i in range(taps):
                        term = short[taps * j + i] * ds[j][i]
                        dn = term if dn is None else dn + term
                weighted = gain * dn
                wd[here, :] = weighted
                spot = pl.multiple_of((g * total + w) * SUB, SUB)
                parts[pl.ds(spot, SUB), :] = xh * weighted
                if acc is not None:
                    product, normed = key * value, xh * gain
                    fresh = [acc[0] + xh * dn]
                    for j in range(3):
                        for i in range(taps):
                            fresh.append(acc[1 + taps * j + i] + normed * ds[j][i])
                    for i in range(nlong):
                        fresh.append(acc[1 + nshort + i] + product * dmix[i])
                    acc = fresh
                return (dmix[:-1], [d[:-1] for d in ds]), acc

            def flat(state):
                return tuple(state[0]) + tuple(v for d in state[1] for v in d)

            def unflat(vals):
                n = nlong - 1
                rest = vals[n:]
                m = taps - 1
                return list(vals[:n]), [list(rest[j * m : (j + 1) * m]) for j in range(3)]

            nstate = nlong - 1 + 3 * (taps - 1)

            def warm(it, carry):
                state = unflat(carry)
                for u in range(unroll):
                    state, _ = one(top - 1 - it * unroll - u, state, None)
                return flat(state)

            def main(it, carry):
                state, acc = unflat(carry[:nstate]), list(carry[nstate:])
                for u in range(unroll):
                    state, acc = one(halo + nrow - 1 - it * unroll - u, state, acc)
                return flat(state) + tuple(acc)

            zero = blank[...]
            carry = lax.fori_loop(0, (top - halo - nrow) // unroll, warm, (zero,) * nstate)
            carry = lax.fori_loop(0, nrow // unroll, main, carry + (zero,) * ntap)
            for k in range(ntap):
                grads[pl.ds(pl.multiple_of(k * nb + g * SUB, SUB), SUB), :] = carry[nstate + k]
            return 0

        lax.fori_loop(0, groups, group, 0)

    def split_grads(b):
        for z in range(nctx):
            for k in range(ntap):
                gs[b, z, k * cb : (k + 1) * cb, :] = grads[k * nb + z * cb : k * nb + (z + 1) * cb, :]

    def mean_of(value):
        return value / width

    backward(1, total, 4)
    send_stat(2, collect(halo // SUB, nstat))
    split_grads(1)
    grad_sends = []
    for o in range(nctx):
        z = ctx_at(o)
        grad_sends.append(
            remote(gs.at[1, z], rg.at[1, ctx], g_send.at[1, o], g_recv.at[1, ctx], dev(follow, z, dp))
        )
        grad_sends[-1].start()
    unpack(2, get_stat(2), mean_of)

    backward(0, halo + nrow + halo // 2, 4)
    send_stat(3, collect(halo // SUB, (halo + nrow) // SUB))
    split_grads(0)
    for o in range(1, nctx):
        z = ctx_at(o)
        grad_sends.append(
            remote(gs.at[0, z], rg.at[0, ctx], g_send.at[0, o], g_recv.at[0, ctx], dev(pipe, z, dp))
        )
        grad_sends[-1].start()
    rg[0, ctx] = gs[0, ctx]
    unpack(3, get_stat(3), mean_of)

    def finish(i, _):
        w = halo + i * 16
        halves = [pl.multiple_of(w + half * SUB, SUB) for half in range(2)]
        scales = [rows[0, pl.ds(h, SUB), :] for h in halves]
        means = [rows[3, pl.ds(h, SUB), :] for h in halves]
        for j in range(nb):
            pieces = []
            for half in range(2):
                here = pl.ds(halves[half] * nb + j, SUB, stride=nb)
                pieces.append(zs[here, :] + scales[half] * (wd[here, :] - saved[0, 0, here, :] * means[half]))
            out[0, pl.ds(pl.multiple_of(i * 16, 16), 16), j * LANES : (j + 1) * LANES] = jnp.concatenate(
                pieces, axis=0
            ).astype(BF16)
        return 0

    lax.fori_loop(0, nrow // 16, finish, 0)

    for z in range(nctx):
        remote(gs.at[1, z], rg.at[1, z], g_send.at[1, z], g_recv.at[1, z], dev(prev, z, dp)).wait_recv()
    for o in range(1, nctx):
        z = ctx_at(o)
        remote(gs.at[0, z], rg.at[0, z], g_send.at[0, o], g_recv.at[0, z], dev(pipe, z, dp)).wait_recv()
    result = rg[0, 0] + rg[1, 0]
    for z in range(1, nctx):
        result = result + (rg[0, z] + rg[1, z])
    for k in range(ntap):
        for j in range(cb):
            cols = pl.ds(j * LANES, LANES)
            piece = result[k * cb + j : k * cb + j + 1, :]
            if k == 0:
                gain_out[0:1, cols] = piece
            elif k <= nshort:
                short_out[0, k - 1 : k, cols] = piece
            else:
                long_out[0, k - 1 - nshort : k - nshort, cols] = piece

    @pl.when(has_up)
    def _():
        to_bot.wait_send()
        to_cbot.wait_send()

    @pl.when(has_down)
    def _():
        to_top.wait_send()

    to_cot.wait_send()
    for c in own_sends + grad_sends:
        c.wait_send()


def per_device(mesh, hidden, cotangent, gain_rows, short_taps, long_taps):
    npipe, nctx, ndp = mesh.shape["pipe"], mesh.shape["ctx"], mesh.shape["dp"]
    nrow, chans = hidden.shape[1], hidden.shape[2]
    own = gain_rows.shape[1]
    wide = -(-own // LANES) * LANES
    nshort, nlong = short_taps.shape[1], long_taps.shape[1]
    ntap = 1 + nshort + nlong
    cb = wide // LANES
    nb = nctx * cb
    halo = 2 * (nshort // 3 + nlong - 2)
    total = nrow + 2 * halo
    slab_rows = -(-ntap * cb // SUB) * SUB

    def widen(values):
        if wide == own:
            return values
        lead = values.shape[:-1]
        blocks = values.reshape(lead + (-1, own))
        blocks = jnp.pad(blocks, [(0, 0)] * (len(lead) + 1) + [(0, wide - own)])
        return blocks.reshape(lead + (-1,))

    def narrow(values):
        if wide == own:
            return values
        lead = values.shape[:-1]
        return values.reshape(lead + (-1, wide))[..., :own].reshape(lead + (-1,))

    cfg = dict(
        npipe=npipe, nctx=nctx, ndp=ndp, nrow=nrow, nb=nb, cb=cb, ntap=ntap, nshort=nshort,
        width=float(chans * ndp), halo=halo,
    )
    full = nb * LANES
    dma = pltpu.SemaphoreType.DMA
    vmem = pl.BlockSpec(memory_space=pltpu.VMEM)
    anywhere = pl.BlockSpec(memory_space=pl.ANY)
    outs = pl.pallas_call(
        functools.partial(kernel, cfg),
        out_shape=(
            jax.ShapeDtypeStruct((1, nrow, full), BF16),
            jax.ShapeDtypeStruct((1, wide), F32),
            jax.ShapeDtypeStruct((1, nshort, wide), F32),
            jax.ShapeDtypeStruct((1, nlong, wide), F32),
        ),
        in_specs=[anywhere, anywhere, vmem, vmem, vmem],
        out_specs=(vmem, vmem, vmem, vmem),
        scratch_shapes=[
            pltpu.VMEM((nrow, full), BF16),
            pltpu.VMEM((halo, full), BF16),
            pltpu.VMEM((halo, full), BF16),
            pltpu.VMEM((nrow, full), BF16),
            pltpu.VMEM((halo, full), BF16),
            pltpu.VMEM((slab_rows, LANES), F32),
            pltpu.VMEM((2, nctx, slab_rows, LANES), F32),
            pltpu.VMEM((2, ntap * nb, LANES), F32),
            pltpu.VMEM((ntap * nb, LANES), F32),
            pltpu.VMEM((2, nctx, slab_rows, LANES), F32),
            pltpu.VMEM((2, nctx, slab_rows, LANES), F32),
            pltpu.VMEM((total * nb, LANES), F32),
            pltpu.VMEM((total * nb, LANES), F32),
            pltpu.VMEM((total * nb, LANES), F32),
            pltpu.VMEM((2, 5, total * nb, LANES), F32),
            pltpu.VMEM((total * nb, LANES), F32),
            pltpu.VMEM((4, SUB, LANES), F32),
            pltpu.VMEM((4, ndp, SUB, LANES), F32),
            pltpu.VMEM((4, total, LANES), F32),
            pltpu.VMEM((SUB, LANES), F32),
            dma((1,)),
            dma((4,)),
            dma((4,)),
            dma((2, nctx)),
            dma((2, nctx)),
            dma((2, nctx)),
            dma((2, nctx)),
            dma((4, ndp)),
            dma((4, ndp)),
        ],
        compiler_params=pltpu.CompilerParams(
            collective_id=0, has_side_effects=True, vmem_limit_bytes=56 * 1024 * 1024
        ),
        name="relay",
    )(widen(hidden), widen(cotangent), widen(gain_rows), widen(short_taps), widen(long_taps))
    return tuple(narrow(o) for o in outs)


def solution(mesh):
    in_specs = (
        P("pipe", "ctx", "dp"),
        P("pipe", "ctx", "dp"),
        P("pipe", ("dp", "ctx")),
        P("pipe", None, ("dp", "ctx")),
        P("pipe", None, ("dp", "ctx")),
    )
    out_specs = (
        P("pipe", "ctx", "dp"),
        P("pipe", ("dp", "ctx")),
        P("pipe", None, ("dp", "ctx")),
        P("pipe", None, ("dp", "ctx")),
    )
    return jax.shard_map(
        functools.partial(per_device, mesh), mesh=mesh, in_specs=in_specs, out_specs=out_specs, check_vma=False
    )
```

time: 189 us -> 69.2 us (0.37)
  waiting for transfers between devices: 64.3 us -> 0 us
  Pallas kernels: 0 us -> 61.4 us
  other arithmetic: 56.5 us -> 0 us
  blocking collectives: 34.2 us -> 0 us
  between operations: 14.5 us -> 0.66 us
  starting transfers between devices: 9.22 us -> 0 us
  local copies, waits for them, and re-layouts: 9.25 us -> 6.8 us
    pallas_call x0 -> x1, Pallas kernels: none -> 61.4 us  [per_device(): pl.pallas_call(functools.partial(kernel, cfg), out_shape=(jax.ShapeDtypeS...]
    ppermute x6 -> x0, waiting for transfers between devices: 48.8 us -> none  [the longest x2 37.8 us: shifted(): return lax.ppermute(value, axis, pairs)]
    reduce_sum x8 -> x0, other arithmetic: 28.2 us -> none  [the longest x2 14 us: conv_branch(): short_filter[tap_count * stream_index + tap_index] * lagged[tap_index]]
    psum x4 -> x0, blocking collectives: 19.9 us -> none  [row_total(): return lax.psum(values, 'dp')]
    reduce_scatter x1 -> x0, waiting for transfers between devices: 15.5 us -> none  [per_device(): lax.psum_scatter(summed_grads, 'ctx', scatter_dimension=1, tiled=True)]
    all_gather x1 -> x0, blocking collectives: 14.3 us -> none  [per_device(): filters = lax.all_gather(packed, 'ctx', axis=1, tiled=True)]
    mul x15 -> x0, other arithmetic: 10.4 us -> none  [the longest x12 8.45 us: conv_branch(): mixing = mixing + long_filter[tap_index] * delayed(product, tap_index)]
    ppermute x6 -> x0, starting transfers between devices: 9.18 us -> none  [the longest x4 8.9 us: passed_along(): lax.ppermute(value, axis, [(source, source + steps) for source in range(i...]
  transfers between devices with their start and end apart: 7 -> 0, of which waited for: 6 -> 0; matrix products, arithmetic and copies ran while one was open for 3% -> 0% of each run, Pallas kernels for 0% -> 0%
where the time goes in v1:
time: 69.2 us; the launch traced here: 68.8 us
  Pallas kernels  61.4 us (89%)
  local copies, waits for them, and re-layouts  6.8 us (10%)
    pallas_call x1, Pallas kernels, per_device(): pl.pallas_call(functools.partial(kernel, cfg), out_shape=(jax.ShapeDtypeS...  61.4 us
    unnamed x10, local copies, waits for them, and re-layouts  4.84 us
    pallas_call x2, local copies, waits for them, and re-layouts, per_device(): pl.pallas_call(functools.partial(kernel, cfg), out_shape=(jax.ShapeDtypeS...  1.96 us

profile of v1, /device:TPU:0, one launch (start us, length us, event | category | flops | bytes accessed | tf_op | source)
XLA Modules:
  0.0 68.8 jit_solution(15466350593246573137)
XLA Ops:
  0.6 0.0 copy-start.1
  0.6 1.3 %copy.10.long_in = f32[1,7,512]{2,1,0:T(8,128)} copy(f32[1,7,512]{2,0,1:T(1,128)} %param.9) | data formatting | bytes 28672 | tf_op args[4]
  2.0 0.0 copy-done.1
  2.0 0.6 copy.9.short_in
  2.6 61.4 %relay.1 = (bf16[1,256,2048]{2,1,0:T(8,128)(2,1)}, f32[1,512]{1,0:T(1,128)}, f32[1,9,512]{2,1,0:T(8,128)}, f32[1,7,512]{2,1,0:T(8,128)}) custom-call(bf16[1,256,2048]{2,1,0:T(8,128)(2,1)} %hid.1, bf16[1,256,2048]{2,1,0:T(8,128)(2,1)} %cot.1, f32[1,512]{1,0:T(1,128)} %gain_in.1, f32[1,9,512]{2,1,0:T(8,128)} %copy.9.short_in, f32[1,7,512]{2,1,0:T(8,128)} %copy.10.long_in), custom_call_target="tpu_custom_call" | custom-call | tf_op jit(solution)/shard_map/relay/pallas_call | solution.py:515
  63.9 0.0 copy-start
  64.0 1.3 %copy.12 = f32[1,7,512]{2,0,1:T(1,128)} copy(f32[1,7,512]{2,1,0:T(8,128)} %get-tuple-element.7) | data formatting | bytes 28672 | tf_op jit(solution)/shard_map/relay/pallas_call | solution.py:515
  65.3 0.0 copy-done
  65.3 0.6 copy.11
  65.9 0.0 copy-start.2
  65.9 2.3 %copy.15 = bf16[1,256,2048]{2,1,0:T(8,128)(2,1)} copy(bf16[1,256,2048]{2,1,0:T(8,128)(2,1)} %get-tuple-element.12) | data formatting | bytes 2097152
  68.2 0.0 copy-done.2
  68.2 0.6 copy.16
Async XLA Ops:
  0.6 1.3 %copy-start.1 = (f32[1,9,512]{2,0,1:T(1,128)S(1)}, f32[1,9,512]{2,0,1:T(1,128)}, u32[]{:S(2)}) copy-start(f32[1,9,512]{2,0,1:T(1,128)} %param.8) | copy-start | bytes 55300
  63.9 1.4 %copy-start = (f32[1,9,512]{2,1,0:T(8,128)S(1)}, f32[1,9,512]{2,1,0:T(8,128)}, u32[]{:S(2)}) copy-start(f32[1,9,512]{2,1,0:T(8,128)} %get-tuple-element.6) | copy-start | bytes 55300
  65.9 2.3 %copy-start.2 = (f32[1,512]{1,0:T(1,128)S(1)}, f32[1,512]{1,0:T(1,128)}, u32[]{:S(2)}) copy-start(f32[1,512]{1,0:T(1,128)} %get-tuple-element.13) | copy-start | bytes 6148

commit v2 on v1

--- a/solution.py
+++ b/solution.py
@@ -38,8 +38,10 @@
     gs,
     rg,
     xs,
+    ys,
     zs,
-    wd,
+    wd_outer,
+    wd_inner,
     saved,
     parts,
     st_send,
@@ -92,7 +94,7 @@
         src, row = (gain_in, 0) if k == 0 else ((short_in, k - 1) if k <= nshort else (long_in, k - 1 - nshort))
         for j in range(cb):
             cols = pl.ds(j * LANES, LANES)
-            piece = src[row : row + 1, cols] if k == 0 else src[0, row : row + 1, cols]
+            piece = src[row : row + 1, cols] if k == 0 else src[row, 0:1, cols]
             slab[k * cb + j : k * cb + j + 1, :] = piece
     pad = slab.shape[0] - ntap * cb
     if pad:
@@ -235,7 +237,7 @@
                     acc = piece if acc is None else acc + piece
             return jnp.where(lane == i, jnp.sum(acc, axis=1, keepdims=True), stat)
 
-        return lax.fori_loop(lo, hi, step, jnp.zeros((SUB, LANES), F32))
+        return lax.fori_loop(lo, hi, step, jnp.zeros((SUB, LANES), F32), unroll=6)
 
     def build_filters(b):
         for z in range(nctx):
@@ -271,7 +273,7 @@
                 past = list(carry[taps - 1 :])
                 for u in range(unroll):
                     w = lo + it * unroll + u
-                    x = xs[at(w, g), :]
+                    x = (xs if b == 0 else ys)[at(w, g), :]
                     xh = x * row_of(b, w)
                     seq = [xh * gain] + lag
                     streams = []
@@ -288,7 +290,7 @@
                         saved[b, n, at(w, g), :] = value
                     if b == 0:
                         inner = (x + streams[0] * mix).astype(BF16).astype(F32)
-                        xs[at(w, g), :] = inner
+                        ys[at(w, g), :] = inner
                         spot = pl.multiple_of((g * total + w) * SUB, SUB)
                         parts[pl.ds(spot, SUB), :] = inner * inner
                     lag, past = seq[:-1], products[:-1]
@@ -303,28 +305,29 @@
     forward(0, 0, 8)
     send_stat(1, collect(0, nstat))
 
-    remote(cbuf, cbuf, halo_send.at[3], halo_recv.at[3], dev(follow, ctx, dp)).wait_recv()
-
-    @pl.when(has_down)
-    def _():
-        remote(cbot, cbot, halo_send.at[2], halo_recv.at[2], dev(follow, down_z, dp)).wait_recv()
-
-    @pl.when(jnp.logical_not(has_down))
-    def _():
-        cbot[...] = jnp.zeros(cbot.shape, BF16)
-
-    def take_cot(i, _):
-        spread(zs, halo + i * 16, cbuf[pl.ds(pl.multiple_of(i * 16, 16), 16), :].astype(F32))
-        return 0
-
-    lax.fori_loop(0, nrow // 16, take_cot, 0)
-    spread(zs, halo + nrow, cbot[...].astype(F32))
     for z in range(nctx):
         remote(slab, fr.at[1, z], f_send.at[1, z], f_recv.at[1, z], dev(follow, z, dp)).wait_recv()
     build_filters(1)
     unpack(1, get_stat(1), row_scale)
     forward(1, halo // 2, 8)
 
+    remote(cbuf, cbuf, halo_send.at[3], halo_recv.at[3], dev(follow, ctx, dp)).wait_recv()
+
+    @pl.when(has_down)
+    def _():
+        remote(cbot, cbot, halo_send.at[2], halo_recv.at[2], dev(follow, down_z, dp)).wait_recv()
+
+    @pl.when(jnp.logical_not(has_down))
+    def _():
+        cbot[...] = jnp.zeros(cbot.shape, BF16)
+
+    def take_cot(i, _):
+        spread(zs, halo + i * 16, cbuf[pl.ds(pl.multiple_of(i * 16, 16), 16), :].astype(F32))
+        return 0
+
+    lax.fori_loop(0, nrow // 16, take_cot, 0)
+    spread(zs, halo + nrow, cbot[...].astype(F32))
+
     def backward(b, top, unroll):
         def group(g, _):
             fl = [tap(b, k, g) for k in range(ntap)]
@@ -335,8 +338,8 @@
                 here = at(w, g)
                 up = zs[here, :]
                 if b == 0:
-                    up = up + row_of(1, w) * (wd[here, :] - saved[1, 0, here, :] * row_of(2, w))
-                    zs[here, :] = up
+                    up = up + row_of(1, w) * (wd_outer[here, :] - saved[1, 0, here, :] * row_of(2, w))
+                    xs[here, :] = up
                 xh, query, key, value, mix = [saved[b, n, here, :] for n in range(5)]
                 dmix = [up * query] + dmix_next
                 dprod = long[0] * dmix[0]
@@ -349,7 +352,7 @@
                         term = short[taps * j + i] * ds[j][i]
                         dn = term if dn is None else dn + term
                 weighted = gain * dn
-                wd[here, :] = weighted
+                (wd_outer if b == 1 else wd_inner)[here, :] = weighted
                 spot = pl.multiple_of((g * total + w) * SUB, SUB)
                 parts[pl.ds(spot, SUB), :] = xh * weighted
                 if acc is not None:
@@ -436,7 +439,7 @@
             pieces = []
             for half in range(2):
                 here = pl.ds(halves[half] * nb + j, SUB, stride=nb)
-                pieces.append(zs[here, :] + scales[half] * (wd[here, :] - saved[0, 0, here, :] * means[half]))
+                pieces.append(xs[here, :] + scales[half] * (wd_inner[here, :] - saved[0, 0, here, :] * means[half]))
             out[0, pl.ds(pl.multiple_of(i * 16, 16), 16), j * LANES : (j + 1) * LANES] = jnp.concatenate(
                 pieces, axis=0
             ).astype(BF16)
@@ -459,9 +462,9 @@
             if k == 0:
                 gain_out[0:1, cols] = piece
             elif k <= nshort:
-                short_out[0, k - 1 : k, cols] = piece
+                short_out[k - 1, 0:1, cols] = piece
             else:
-                long_out[0, k - 1 - nshort : k - nshort, cols] = piece
+                long_out[k - 1 - nshort, 0:1, cols] = piece
 
     @pl.when(has_up)
     def _():
@@ -475,6 +478,20 @@
     to_cot.wait_send()
     for c in own_sends + grad_sends:
         c.wait_send()
+
+
+def handed_on(a0, a1, a2, a3, b0, b1, b2, b3):
+    b0[...] = a0[...]
+
+    @pl.when(pl.program_id(0) == 0)
+    def _():
+        b1[...] = a1[...]
+        b2[...] = a2[...]
+        b3[...] = a3[...]
+
+
+def swap(values):
+    return jnp.transpose(values, (1, 0, 2))
 
 
 def per_device(mesh, hidden, cotangent, gain_rows, short_taps, long_taps):
@@ -512,14 +529,15 @@
     dma = pltpu.SemaphoreType.DMA
     vmem = pl.BlockSpec(memory_space=pltpu.VMEM)
     anywhere = pl.BlockSpec(memory_space=pl.ANY)
+    shapes = (
+        jax.ShapeDtypeStruct((1, nrow, full), BF16),
+        jax.ShapeDtypeStruct((1, wide), F32),
+        jax.ShapeDtypeStruct((nshort, 1, wide), F32),
+        jax.ShapeDtypeStruct((nlong, 1, wide), F32),
+    )
     outs = pl.pallas_call(
         functools.partial(kernel, cfg),
-        out_shape=(
-            jax.ShapeDtypeStruct((1, nrow, full), BF16),
-            jax.ShapeDtypeStruct((1, wide), F32),
-            jax.ShapeDtypeStruct((1, nshort, wide), F32),
-            jax.ShapeDtypeStruct((1, nlong, wide), F32),
-        ),
+        out_shape=shapes,
         in_specs=[anywhere, anywhere, vmem, vmem, vmem],
         out_specs=(vmem, vmem, vmem, vmem),
         scratch_shapes=[
@@ -534,6 +552,8 @@
             pltpu.VMEM((ntap * nb, LANES), F32),
             pltpu.VMEM((2, nctx, slab_rows, LANES), F32),
             pltpu.VMEM((2, nctx, slab_rows, LANES), F32),
+            pltpu.VMEM((total * nb, LANES), F32),
+            pltpu.VMEM((total * nb, LANES), F32),
             pltpu.VMEM((total * nb, LANES), F32),
             pltpu.VMEM((total * nb, LANES), F32),
             pltpu.VMEM((total * nb, LANES), F32),
@@ -557,8 +577,19 @@
             collective_id=0, has_side_effects=True, vmem_limit_bytes=56 * 1024 * 1024
         ),
         name="relay",
-    )(widen(hidden), widen(cotangent), widen(gain_rows), widen(short_taps), widen(long_taps))
-    return tuple(narrow(o) for o in outs)
+    )(widen(hidden), widen(cotangent), widen(gain_rows), swap(widen(short_taps)), swap(widen(long_taps)))
+    passed = [pl.BlockSpec((1, nrow // 4, full), lambda i: (0, i, 0))] + [
+        pl.BlockSpec(o.shape, functools.partial(lambda rank, i: (0,) * rank, len(o.shape))) for o in shapes[1:]
+    ]
+    outs = pl.pallas_call(
+        handed_on,
+        out_shape=shapes,
+        grid=(4,),
+        in_specs=passed,
+        out_specs=tuple(passed),
+        name="handed_on",
+    )(*outs)
+    return tuple(narrow(o) for o in (outs[0], outs[1], swap(outs[2]), swap(outs[3])))
 
 
 def solution(mesh):

time: 69.2 us -> 54.2 us (0.78)
  Pallas kernels: 61.4 us -> 53.4 us
  local copies, waits for them, and re-layouts: 6.8 us -> 0 us
    pallas_call x1 -> x2, Pallas kernels: 61.4 us -> 53.4 us  [the longest x1 50 us: per_device(): pl.pallas_call(functools.partial(kernel, cfg), out_shape=shapes, in_specs...]
    unnamed x10 -> x0, local copies, waits for them, and re-layouts: 4.84 us -> none
    pallas_call x2 -> x0, local copies, waits for them, and re-layouts: 1.96 us -> none  [per_device(): pl.pallas_call(functools.partial(kernel, cfg), out_shape=(jax.ShapeDtypeS...]
where the time goes in v2:
time: 54.2 us; the launch traced here: 54 us
  Pallas kernels  53.4 us (99%)
  between operations  0.64 us (1%)
    pallas_call x1, Pallas kernels, per_device(): pl.pallas_call(functools.partial(kernel, cfg), out_shape=shapes, in_specs...  50 us
    pallas_call x1, Pallas kernels, per_device(): pl.pallas_call(handed_on, out_shape=shapes, grid=(4,), in_specs=passed, o...  3.4 us

profile of v2, /device:TPU:0, one launch (start us, length us, event | category | flops | bytes accessed | tf_op | source)
XLA Modules:
  0.0 54.0 jit_solution(16258117532630598538)
XLA Ops:
  0.6 50.0 %relay.1 = (bf16[1,256,2048]{2,1,0:T(8,128)(2,1)}, f32[1,512]{1,0:T(1,128)}, f32[9,1,512]{2,1,0:T(1,128)}, f32[7,1,512]{2,1,0:T(1,128)}) custom-call(bf16[1,256,2048]{2,1,0:T(8,128)(2,1)} %hid.1, bf16[1,256,2048]{2,1,0:T(8,128)(2,1)} %cot.1, f32[1,512]{1,0:T(1,128)} %gain_in.1, f32[9,1,512]{2,1,0:T(1,128)} %bitcast.4, f32[7,1,512]{2,1,0:T(1,128)} %bitcast.5), custom_call_target="tpu_custom_call" | custom-call | tf_op jit(solution)/shard_map/relay/pallas_call | solution.py:538
  50.6 3.4 %handed_on.1 = (bf16[1,256,2048]{2,1,0:T(8,128)(2,1)}, f32[1,512]{1,0:T(1,128)}, f32[9,1,512]{2,1,0:T(1,128)}, f32[7,1,512]{2,1,0:T(1,128)}) custom-call(bf16[1,256,2048]{2,1,0:T(8,128)(2,1)} %get-tuple-element.12.a0, f32[1,512]{1,0:T(1,128)} %get-tuple-element.13.a1, f32[9,1,512]{2,1,0:T(1,128)} %get-tuple-element.14.a2, f32[7,1,512]{2,1,0:T(1,128)} %get-tuple-element.15.a3), custom_call_target="tpu_custom_call" | custom-call | tf_op jit(solution)/shard_map/handed_on/pallas_call | solution.py:584

commit v3 on v2

--- a/solution.py
+++ b/solution.py
@@ -406,7 +406,7 @@
     def mean_of(value):
         return value / width
 
-    backward(1, total, 4)
+    backward(1, total, 8)
     send_stat(2, collect(halo // SUB, nstat))
     split_grads(1)
     grad_sends = []
@@ -418,7 +418,7 @@
         grad_sends[-1].start()
     unpack(2, get_stat(2), mean_of)
 
-    backward(0, halo + nrow + halo // 2, 4)
+    backward(0, halo + nrow + halo // 2, 8)
     send_stat(3, collect(halo // SUB, (halo + nrow) // SUB))
     split_grads(0)
     for o in range(1, nctx):
@@ -578,13 +578,13 @@
         ),
         name="relay",
     )(widen(hidden), widen(cotangent), widen(gain_rows), swap(widen(short_taps)), swap(widen(long_taps)))
-    passed = [pl.BlockSpec((1, nrow // 4, full), lambda i: (0, i, 0))] + [
+    passed = [pl.BlockSpec((1, nrow // 2, full), lambda i: (0, i, 0))] + [
         pl.BlockSpec(o.shape, functools.partial(lambda rank, i: (0,) * rank, len(o.shape))) for o in shapes[1:]
     ]
     outs = pl.pallas_call(
         handed_on,
         out_shape=shapes,
-        grid=(4,),
+        grid=(2,),
         in_specs=passed,
         out_specs=tuple(passed),
         name="handed_on",

time: 54.2 us -> 51.1 us (0.943)
  Pallas kernels: 53.4 us -> 50.2 us
    pallas_call x1, Pallas kernels: 50 us -> 48.1 us  [per_device(): pl.pallas_call(functools.partial(kernel, cfg), out_shape=shapes, in_specs...]
    pallas_call x1, Pallas kernels: 3.4 us -> 2.1 us  [per_device(): pl.pallas_call(handed_on, out_shape=shapes, grid=(2,), in_specs=passed, o...]
where the time goes in v3:
time: 51.1 us; the launch traced here: 50.8 us
  Pallas kernels  50.2 us (98%)
  between operations  0.64 us (1%)
    pallas_call x1, Pallas kernels, per_device(): pl.pallas_call(functools.partial(kernel, cfg), out_shape=shapes, in_specs...  48.1 us
    pallas_call x1, Pallas kernels, per_device(): pl.pallas_call(handed_on, out_shape=shapes, grid=(2,), in_specs=passed, o...  2.1 us

profile of v3, /device:TPU:0, one launch (start us, length us, event | category | flops | bytes accessed | tf_op | source)
XLA Modules:
  0.0 50.8 jit_solution(9141954846978780691)
XLA Ops:
  0.6 48.1 %relay.1 = (bf16[1,256,2048]{2,1,0:T(8,128)(2,1)}, f32[1,512]{1,0:T(1,128)}, f32[9,1,512]{2,1,0:T(1,128)}, f32[7,1,512]{2,1,0:T(1,128)}) custom-call(bf16[1,256,2048]{2,1,0:T(8,128)(2,1)} %hid.1, bf16[1,256,2048]{2,1,0:T(8,128)(2,1)} %cot.1, f32[1,512]{1,0:T(1,128)} %gain_in.1, f32[9,1,512]{2,1,0:T(1,128)} %bitcast.4, f32[7,1,512]{2,1,0:T(1,128)} %bitcast.5), custom_call_target="tpu_custom_call" | custom-call | tf_op jit(solution)/shard_map/relay/pallas_call | solution.py:538
  48.7 2.1 %handed_on.1 = (bf16[1,256,2048]{2,1,0:T(8,128)(2,1)}, f32[1,512]{1,0:T(1,128)}, f32[9,1,512]{2,1,0:T(1,128)}, f32[7,1,512]{2,1,0:T(1,128)}) custom-call(bf16[1,256,2048]{2,1,0:T(8,128)(2,1)} %get-tuple-element.12.a0, f32[1,512]{1,0:T(1,128)} %get-tuple-element.13.a1, f32[9,1,512]{2,1,0:T(1,128)} %get-tuple-element.14.a2, f32[7,1,512]{2,1,0:T(1,128)} %get-tuple-element.15.a3), custom_call_target="tpu_custom_call" | custom-call | tf_op jit(solution)/shard_map/handed_on/pallas_call | solution.py:584
